TPU v7x, 32 devices: a whole 2x2x4 slice. The times are simulated.
32 devices in a mesh: dp: 8 (over y, x, core), tensor: 4 (over z).
Axes of the slice: x: 2, y: 2, z: 4, core: 2. Of those that a mesh axis runs over, the one named last changes fastest.
Arguments:
- tokens: bfloat16 [16, 577, 1024], P('dp', None, 'tensor'), may hold values from -6 to 6
- cotangent: float32 [16, 577, 1024], P('dp', None, 'tensor'), may hold values from -6 to 6
- image_counts: int32 [8], P('dp'), may hold values from 1 to 2, as said below
- w_qkv: float32 [2, 1024, 3, 1024], P(None, 'dp', None, 'tensor'), as said below
- w_out: float32 [2, 1024, 1024], P(None, 'dp', 'tensor'), may hold values from -0.75 to 0.75
- w_fc1: float32 [2, 1024, 4096], P(None, 'dp', 'tensor'), may hold values from -0.1875 to 0.1875
- w_fc2: float32 [2, 1024, 4096], P(None, 'dp', 'tensor'), may hold values from -0.09375 to 0.09375
- vec_small: float32 [2, 8, 1024], P(None, None, 'tensor'), as said below
- fc1_bias: float32 [2, 4096], P(None, 'tensor'), may hold values from -3 to 3
- mom_qkv: float32 [2, 2, 1024, 3, 1024], P(None, None, 'dp', None, 'tensor'), as said below
- mom_out: float32 [2, 2, 1024, 1024], P(None, None, 'dp', 'tensor'), as said below
- mom_fc1: float32 [2, 2, 1024, 4096], P(None, None, 'dp', 'tensor'), as said below
- mom_fc2: float32 [2, 2, 1024, 4096], P(None, None, 'dp', 'tensor'), as said below
- mom_vec: float32 [2, 2, 8, 1024], P(None, None, None, 'tensor'), as said below
- mom_bias: float32 [2, 2, 4096], P(None, None, 'tensor'), as said below
Outputs:
- output: float32 [16, 577, 1024], P('dp', None, 'tensor')
- input_grad: float32 [16, 577, 1024], P('dp', None, 'tensor')
- grad_qkv: float32 [2, 1024, 3, 1024], P(None, 'dp', None, 'tensor')
- grad_out: float32 [2, 1024, 1024], P(None, 'dp', 'tensor')
- grad_fc1: float32 [2, 1024, 4096], P(None, 'dp', 'tensor')
- grad_fc2: float32 [2, 1024, 4096], P(None, 'dp', 'tensor')
- grad_vec: float32 [2, 8, 1024], P(None, None, 'tensor')
- grad_bias: float32 [2, 4096], P(None, 'tensor')
- new_qkv: float32 [2, 1024, 3, 1024], P(None, 'dp', None, 'tensor')
- new_out: float32 [2, 1024, 1024], P(None, 'dp', 'tensor')
- new_fc1: float32 [2, 1024, 4096], P(None, 'dp', 'tensor')
- new_fc2: float32 [2, 1024, 4096], P(None, 'dp', 'tensor')
- new_vec: float32 [2, 8, 1024], P(None, None, 'tensor')
- new_bias: float32 [2, 4096], P(None, 'tensor')
- newmom_qkv: float32 [2, 2, 1024, 3, 1024], P(None, None, 'dp', None, 'tensor')
- newmom_out: float32 [2, 2, 1024, 1024], P(None, None, 'dp', 'tensor')
- newmom_fc1: float32 [2, 2, 1024, 4096], P(None, None, 'dp', 'tensor')
- newmom_fc2: float32 [2, 2, 1024, 4096], P(None, None, 'dp', 'tensor')
- newmom_vec: float32 [2, 2, 8, 1024], P(None, None, None, 'tensor')
- newmom_bias: float32 [2, 2, 4096], P(None, None, 'tensor')
Inputs may be any that keep to these rules, and one draw needn't show every extreme that they name: Every index of dp holds 1 or 2 images; some index holds 2 and some holds 1. Slot 2 i always holds an image, slot 2 i + 1 only where image_counts[i] is 2; other slots' tokens and cotangents are ignored. `w_qkv`: independent entries of mean 0 and deviation 1024^-0.5. `vec_small`: gains and shifts of order one. `mom_qkv`: second moments (index 1 of dimension 0) are positive. `mom_out`: second moments (index 1 of dimension 0) are positive. `mom_fc1`: second moments (index 1 of dimension 0) are positive. `mom_fc2`: second moments (index 1 of dimension 0) are positive. `mom_vec`: second moments (index 1 of dimension 0) are positive. `mom_bias`: second moments (index 1 of dimension 0) are positive.
All inputs are finite; a program needn't handle non-finite values.
Results may differ from a plain program's by a relative error of at most 0.022.
Values may be sent and summed in bfloat16 or wider, within the bound.
A program may use at most 256 MiB of HBM per device.

v0:
```python
import jax
import jax.numpy as jnp
from jax import lax
from jax.sharding import PartitionSpec as P

D = 1024
HEADS = 16
LAYERS = 2
STEP = 10
NORM_EPS = 1e-06
ROOT_HALF = 0.7071067811865476
INV_ROOT_TWO_PI = 0.3989422804014327
LEARN_RATE = 0.01
BETA_ONE = 0.9
BETA_TWO = 0.999
ADAM_EPS = 1e-08
WEIGHT_DECAY = 0.05
CONTRACT_LAST = (((1,), (1,)), ((), ()))
CONTRACT_FIRST = (((0,), (0,)), ((), ()))


def as_sent(shard):
    return jax.tree.map(lambda a: a.astype(jnp.bfloat16) if a.dtype == jnp.float32 else a, shard)


def gelu_value(preactivation):
    return 0.5 * preactivation * (1.0 + jax.scipy.special.erf(preactivation * ROOT_HALF))


def gelu_slope(preactivation):
    return (
        0.5 * (1.0 + jax.scipy.special.erf(preactivation * ROOT_HALF))
        + preactivation * jnp.exp(-0.5 * preactivation * preactivation) * INV_ROOT_TWO_PI
    )


def layer_statistics(hidden_state):
    totals = lax.psum(
        (jnp.sum(hidden_state, -1), jnp.sum(hidden_state * hidden_state, -1)), "tensor"
    )
    mean_row = totals[0][..., None] / D
    spread = totals[1][..., None] / D - mean_row * mean_row
    inv_std = lax.rsqrt(spread + NORM_EPS)
    return ((hidden_state - mean_row) * inv_std, inv_std)


def norm_back(d_normed, normed, inv_std, gain, carried):
    d_hat = d_normed * gain
    totals = lax.psum((jnp.sum(d_hat, -1), jnp.sum(d_hat * normed, -1)), "tensor")
    grad_in = carried + inv_std * (
        d_hat - totals[0][..., None] / D - normed * totals[1][..., None] / D
    )
    return (grad_in, jnp.sum(d_normed * normed, (0, 1)), jnp.sum(d_normed, (0, 1)))


def share_features(local_rows):
    return lax.all_gather(local_rows, "tensor", axis=2, tiled=True)


def sum_branch(partial_rows):
    return lax.psum_scatter(partial_rows, "tensor", scatter_dimension=2, tiled=True)


def share_grads(local_rows):
    return lax.all_gather(local_rows, "tensor", axis=2, tiled=True)


def sum_inputs(partial_rows):
    return lax.psum_scatter(
        partial_rows.astype(jnp.bfloat16), "tensor", scatter_dimension=2, tiled=True
    ).astype(jnp.float32)


def fetch_weights(w_qkv, w_out, w_fc1, w_fc2, layer_number):
    pieces = (
        w_qkv[layer_number].astype(jnp.bfloat16),
        w_out[layer_number].astype(jnp.bfloat16),
        w_fc1[layer_number].astype(jnp.bfloat16),
        w_fc2[layer_number].astype(jnp.bfloat16),
    )
    return (
        lax.all_gather(pieces[0], "dp", axis=0, tiled=True),
        lax.all_gather(pieces[1], "dp", axis=0, tiled=True),
        lax.all_gather(pieces[2], "dp", axis=0, tiled=True),
        lax.all_gather(pieces[3], "dp", axis=0, tiled=True),
    )


def attend_forward(query_h, key_h, value_h, attn_scale):
    scores = (
        jnp.einsum("bqhd,bkhd->bhqk", query_h, key_h, preferred_element_type=jnp.float32)
        * attn_scale
    )
    top_score = jnp.max(scores, -1, keepdims=True)
    logged_total = top_score + jnp.log(jnp.sum(jnp.exp(scores - top_score), -1, keepdims=True))
    probs = jnp.exp(scores - logged_total).astype(jnp.bfloat16)
    attention_result = jnp.einsum(
        "bhqk,bkhd->bqhd", probs, value_h, preferred_element_type=jnp.float32
    ).astype(jnp.bfloat16)
    return (attention_result, logged_total)


def attend_backward(query_h, key_h, value_h, attention_result, d_att, logged_total, attn_scale):
    scores = (
        jnp.einsum("bqhd,bkhd->bhqk", query_h, key_h, preferred_element_type=jnp.float32)
        * attn_scale
    )
    probs = jnp.exp(scores - logged_total)
    probs_low = probs.astype(jnp.bfloat16)
    d_value = jnp.einsum("bhqk,bqhd->bkhd", probs_low, d_att, preferred_element_type=jnp.float32)
    d_probs = jnp.einsum("bqhd,bkhd->bhqk", d_att, value_h, preferred_element_type=jnp.float32)
    delta = jnp.sum(d_att.astype(jnp.float32) * attention_result.astype(jnp.float32), -1)
    d_scores = (probs * (d_probs - jnp.swapaxes(delta, 1, 2)[..., None]) * attn_scale).astype(
        jnp.bfloat16
    )
    d_query = jnp.einsum("bhqk,bkhd->bqhd", d_scores, key_h, preferred_element_type=jnp.float32)
    d_key = jnp.einsum("bhqk,bqhd->bkhd", d_scores, query_h, preferred_element_type=jnp.float32)
    return (d_query, d_key, d_value)


def adam_update(param, running_gradient, moments, decay):
    first = BETA_ONE * moments[0] + (1.0 - BETA_ONE) * running_gradient
    second = BETA_TWO * moments[1] + (1.0 - BETA_TWO) * running_gradient * running_gradient
    fix_one = 1.0 - BETA_ONE**STEP
    fix_two = 1.0 - BETA_TWO**STEP
    update = first / fix_one / (jnp.sqrt(second / fix_two) + ADAM_EPS) + decay * param
    return (param - LEARN_RATE * update, jnp.stack([first, second]))


def on_device(
    tokens,
    cotangent,
    image_counts,
    w_qkv,
    w_out,
    w_fc1,
    w_fc2,
    vec_small,
    fc1_bias,
    mom_qkv,
    mom_out,
    mom_fc1,
    mom_fc2,
    mom_vec,
    mom_bias,
):
    slot_count, seq_len, feat_width = tokens.shape
    tok_rows = slot_count * seq_len
    heads_here = HEADS // lax.axis_size("tensor")
    head_dim = feat_width // heads_here
    attn_scale = head_dim ** (-0.5)
    slot_live = jnp.stack([jnp.ones((), jnp.float32), (image_counts[0] == 2).astype(jnp.float32)])[
        :, None, None
    ]

    def to_heads(matrix):
        return matrix.reshape(slot_count, seq_len, heads_here, head_dim)

    def to_slots(matrix):
        return matrix.reshape(slot_count, seq_len, -1)

    hidden_state = tokens.astype(jnp.float32)
    saved_tensors = []
    fetched = []
    for layer_number in range(LAYERS):
        weights = fetch_weights(w_qkv, w_out, w_fc1, w_fc2, layer_number)
        fetched.append(weights)
        projection_weight, backward_weight, first_weight, second_weight = weights
        vector_rows = vec_small[layer_number]
        first_centered_scaled, first_inverse_deviation = layer_statistics(hidden_state)
        first_normalized = share_features(
            (first_centered_scaled * vector_rows[0] + vector_rows[1]).astype(jnp.bfloat16)
        ).reshape(tok_rows, -1)
        proj_out = lax.dot_general(
            first_normalized,
            projection_weight,
            (((1,), (0,)), ((), ())),
            preferred_element_type=jnp.float32,
        )
        query_matrix_rows = (proj_out[:, 0] + vector_rows[2]).astype(jnp.bfloat16)
        key_matrix_rows = proj_out[:, 1].astype(jnp.bfloat16)
        value_matrix_rows = (proj_out[:, 2] + vector_rows[3]).astype(jnp.bfloat16)
        attention_result, logged_total = attend_forward(
            to_heads(query_matrix_rows),
            to_heads(key_matrix_rows),
            to_heads(value_matrix_rows),
            attn_scale,
        )
        attention_result = attention_result.reshape(tok_rows, feat_width)
        attn_branch = sum_branch(
            to_slots(
                lax.dot_general(
                    attention_result,
                    backward_weight,
                    CONTRACT_LAST,
                    preferred_element_type=jnp.float32,
                )
            )
        )
        middle_state = hidden_state + attn_branch + vector_rows[4]
        second_centered_scaled, second_inverse_deviation = layer_statistics(middle_state)
        second_normalized = share_features(
            (second_centered_scaled * vector_rows[5] + vector_rows[6]).astype(jnp.bfloat16)
        ).reshape(tok_rows, -1)
        preactivation = (
            jnp.dot(second_normalized, first_weight, preferred_element_type=jnp.float32)
            + fc1_bias[layer_number]
        )
        activation_narrow = gelu_value(preactivation).astype(jnp.bfloat16)
        branch_two = lax.dot_general(
            activation_narrow, second_weight, CONTRACT_LAST, preferred_element_type=jnp.float32
        )
        new_hidden = middle_state + sum_branch(to_slots(branch_two)) + vector_rows[7]
        saved_tensors.append(
            (
                first_centered_scaled,
                first_inverse_deviation,
                first_normalized,
                query_matrix_rows,
                key_matrix_rows,
                value_matrix_rows,
                attention_result,
                logged_total,
                second_centered_scaled,
                second_inverse_deviation,
                second_normalized,
                preactivation,
                activation_narrow,
            )
        )
        hidden_state = new_hidden
    output = hidden_state * slot_live
    running_gradient = cotangent * slot_live
    big_grads = [None] * LAYERS
    vec_grads = [None] * LAYERS
    bias_grads = [None] * LAYERS
    for layer_number in reversed(range(LAYERS)):
        projection_weight, backward_weight, first_weight, second_weight = fetch_weights(
            w_qkv, w_out, w_fc1, w_fc2, layer_number
        )
        vector_rows = vec_small[layer_number]
        (
            first_centered_scaled,
            first_inverse_deviation,
            first_normalized,
            query_matrix_rows,
            key_matrix_rows,
            value_matrix_rows,
            attention_result,
            logged_total,
            second_centered_scaled,
            second_inverse_deviation,
            second_normalized,
            preactivation,
            activation_narrow,
        ) = saved_tensors[layer_number]
        full_grad = share_grads(running_gradient.astype(jnp.bfloat16)).reshape(tok_rows, -1)
        g_fc2 = lax.dot_general(
            full_grad, activation_narrow, CONTRACT_FIRST, preferred_element_type=jnp.float32
        )
        g_bias_two = jnp.sum(running_gradient, (0, 1))
        d_pre = jnp.dot(full_grad, second_weight, preferred_element_type=jnp.float32) * gelu_slope(
            preactivation
        )
        d_pre_low = d_pre.astype(jnp.bfloat16)
        g_fc1 = lax.dot_general(
            second_normalized, d_pre_low, CONTRACT_FIRST, preferred_element_type=jnp.float32
        )
        g_fc1_bias = jnp.sum(d_pre, 0)
        second_normed_gradient = sum_inputs(
            to_slots(
                lax.dot_general(
                    d_pre_low, first_weight, CONTRACT_LAST, preferred_element_type=jnp.float32
                )
            )
        )
        middle_gradient, second_gain_gradient, second_shift_gradient = norm_back(
            second_normed_gradient,
            second_centered_scaled,
            second_inverse_deviation,
            vector_rows[5],
            running_gradient,
        )
        full_mid = share_grads(middle_gradient.astype(jnp.bfloat16)).reshape(tok_rows, -1)
        g_out = lax.dot_general(
            full_mid, attention_result, CONTRACT_FIRST, preferred_element_type=jnp.float32
        )
        g_bias_out = jnp.sum(middle_gradient, (0, 1))
        d_att = jnp.dot(full_mid, backward_weight, preferred_element_type=jnp.float32).astype(
            jnp.bfloat16
        )
        d_query, d_key, d_value = attend_backward(
            to_heads(query_matrix_rows),
            to_heads(key_matrix_rows),
            to_heads(value_matrix_rows),
            to_heads(attention_result),
            to_heads(d_att),
            logged_total,
            attn_scale,
        )
        d_query = d_query.reshape(tok_rows, feat_width)
        d_key = d_key.reshape(tok_rows, feat_width)
        d_value = d_value.reshape(tok_rows, feat_width)
        d_proj = jnp.stack([d_query, d_key, d_value], axis=1).astype(jnp.bfloat16)
        g_qkv = lax.dot_general(
            first_normalized, d_proj, CONTRACT_FIRST, preferred_element_type=jnp.float32
        )
        first_normed_gradient = sum_inputs(
            to_slots(
                lax.dot_general(
                    d_proj,
                    projection_weight,
                    (((1, 2), (1, 2)), ((), ())),
                    preferred_element_type=jnp.float32,
                )
            )
        )
        running_gradient, first_gain_gradient, first_shift_gradient = norm_back(
            first_normed_gradient,
            first_centered_scaled,
            first_inverse_deviation,
            vector_rows[0],
            middle_gradient,
        )
        vec_grads[layer_number] = jnp.stack(
            [
                first_gain_gradient,
                first_shift_gradient,
                jnp.sum(d_query, 0),
                jnp.sum(d_value, 0),
                g_bias_out,
                second_gain_gradient,
                second_shift_gradient,
                g_bias_two,
            ]
        )
        bias_grads[layer_number] = g_fc1_bias
        layer_tuple = (g_qkv, g_out, g_fc1, g_fc2)
        big_grads[layer_number] = layer_tuple
    input_grad = running_gradient * slot_live
    stacked = tuple((jnp.stack([entry[which] for entry in big_grads]) for which in range(4)))
    stacked = jax.tree.map(
        lambda part: part.astype(jnp.float32),
        lax.psum_scatter(as_sent(stacked), "dp", scatter_dimension=1, tiled=True),
    )
    small_sums = lax.psum((jnp.stack(vec_grads), jnp.stack(bias_grads)), "dp")
    grad_totals = (stacked[0], stacked[1], stacked[2], stacked[3], small_sums[0], small_sums[1])
    params = (w_qkv, w_out, w_fc1, w_fc2, vec_small, fc1_bias)
    moments = (mom_qkv, mom_out, mom_fc1, mom_fc2, mom_vec, mom_bias)
    decays = (WEIGHT_DECAY, WEIGHT_DECAY, WEIGHT_DECAY, WEIGHT_DECAY, 0.0, 0.0)
    results = [
        adam_update(param, grad_total, moment, decay)
        for param, grad_total, moment, decay in zip(params, grad_totals, moments, decays)
    ]
    return (
        output,
        input_grad,
        grad_totals[0],
        grad_totals[1],
        grad_totals[2],
        grad_totals[3],
        grad_totals[4],
        grad_totals[5],
        results[0][0],
        results[1][0],
        results[2][0],
        results[3][0],
        results[4][0],
        results[5][0],
        results[0][1],
        results[1][1],
        results[2][1],
        results[3][1],
        results[4][1],
        results[5][1],
    )


def solution(mesh):
    return jax.shard_map(
        on_device,
        mesh=mesh,
        in_specs=(
            P("dp", None, "tensor"),
            P("dp", None, "tensor"),
            P("dp"),
            P(None, "dp", None, "tensor"),
            P(None, "dp", "tensor"),
            P(None, "dp", "tensor"),
            P(None, "dp", "tensor"),
            P(None, None, "tensor"),
            P(None, "tensor"),
            P(None, None, "dp", None, "tensor"),
            P(None, None, "dp", "tensor"),
            P(None, None, "dp", "tensor"),
            P(None, None, "dp", "tensor"),
            P(None, None, None, "tensor"),
            P(None, None, "tensor"),
        ),
        out_specs=(
            P("dp", None, "tensor"),
            P("dp", None, "tensor"),
            P(None, "dp", None, "tensor"),
            P(None, "dp", "tensor"),
            P(None, "dp", "tensor"),
            P(None, "dp", "tensor"),
            P(None, None, "tensor"),
            P(None, "tensor"),
            P(None, "dp", None, "tensor"),
            P(None, "dp", "tensor"),
            P(None, "dp", "tensor"),
            P(None, "dp", "tensor"),
            P(None, None, "tensor"),
            P(None, "tensor"),
            P(None, None, "dp", None, "tensor"),
            P(None, None, "dp", "tensor"),
            P(None, None, "dp", "tensor"),
            P(None, None, "dp", "tensor"),
            P(None, None, None, "tensor"),
            P(None, None, "tensor"),
        ),
        check_vma=False,
    )
```

profile of v0, /device:TPU:0, one launch (start us, length us, event | category | flops | bytes accessed | tf_op | source)
XLA Modules:
  0.0 1669.3 jit_solution(3100951194035109462)
XLA Ops:
  9.8 20.6 %all-reduce.8 = (f32[2,577]{1,0:T(2,128)S(1)}, f32[2,577]{1,0:T(2,128)S(1)}) all-reduce(f32[2,577]{1,0:T(2,128)S(1)} %get-tuple-element.103, f32[2,577]{1,0:T(2,128)S(1)} %get-tuple-element.102), channel_id=1, replica_groups=mesh['dp'=8,'tensor'=4] {'tensor'}, use_global_device_ids=true, to_apply=%region_3.0 | all-reduce | flops 2308 | bytes 18464 | tf_op jit(solution)/shard_map/psum | solution.py:38
  33.9 9.9 all-gather.1
  43.8 38.4 %all-gather.23.cloned.1.call-done = bf16[2,577,1024]{2,1,0:T(8,128)(2,1)} async-done(((bf16[2,577,256]{2,1,0:T(8,128)(2,1)}), bf16[2,577,1024]{2,1,0:T(8,128)(2,1)}) %all-gather.23.cloned.1.call-update) | async-done | bytes 2363408 | tf_op jit(solution)/shard_map/all_gather | solution.py:57
  82.2 3.6 reshape.303
  85.7 22.7 %all-gather.39.cloned.1.call-done = bf16[1,1024,3,256]{3,1,2,0:T(8,128)(2,1)} async-done(((bf16[1,128,3,256]{3,1,2,0:T(8,128)(2,1)}), bf16[1,1024,3,256]{3,1,2,0:T(8,128)(2,1)}) %all-gather.39.cloned.1.call-update) | async-done | bytes 1572880 | tf_op jit(solution)/shard_map/all_gather | solution.py:82
  108.4 4.1 fusion.36
  128.5 3.9 multiply_reduce_fusion.1
  142.3 86.5 %reduce-scatter.13.cloned.1.call-done = f32[2,577,256]{2,1,0:T(8,128)} async-done(((f32[2,577,1024]{2,1,0:T(8,128)}), f32[2,577,256]{2,1,0:T(8,128)}) %reduce-scatter.13.cloned.1.call-update) | async-done | bytes 1181712 | tf_op jit(solution)/shard_map/reduce_scatter | solution.py:61
  230.6 17.9 %all-reduce.7 = (f32[2,577]{1,0:T(2,128)S(1)}, f32[2,577]{1,0:T(2,128)S(1)}) all-reduce(f32[2,577]{1,0:T(2,128)S(1)} %get-tuple-element.93, f32[2,577]{1,0:T(2,128)S(1)} %get-tuple-element.92), channel_id=1, replica_groups=mesh['dp'=8,'tensor'=4] {'tensor'}, use_global_device_ids=true, to_apply=%region_10.0 | all-reduce | flops 2308 | bytes 18464 | tf_op jit(solution)/shard_map/psum | solution.py:38
  253.2 46.1 %all-gather.25.cloned.1.call-done = bf16[2,577,1024]{2,1,0:T(8,128)(2,1)} async-done(((bf16[2,577,256]{2,1,0:T(8,128)(2,1)}), bf16[2,577,1024]{2,1,0:T(8,128)(2,1)}) %all-gather.25.cloned.1.call-update) | async-done | bytes 2363408 | tf_op jit(solution)/shard_map/all_gather | solution.py:57
  299.4 3.6 reshape.282
  302.9 24.7 %all-gather.41.cloned.1.call-done = bf16[1,1024,1024]{2,1,0:T(8,128)(2,1)} async-done(((bf16[1,128,1024]{2,1,0:T(8,128)(2,1)}), bf16[1,1024,1024]{2,1,0:T(8,128)(2,1)}) %all-gather.41.cloned.1.call-update) | async-done | bytes 2097168 | tf_op jit(solution)/shard_map/all_gather | solution.py:84
  327.7 7.1 multiply_convert_fusion.3
  334.8 23.0 %all-gather.43.cloned.1.call-done = bf16[1,1024,1024]{2,1,0:T(8,128)(2,1)} async-done(((bf16[1,128,1024]{2,1,0:T(8,128)(2,1)}), bf16[1,1024,1024]{2,1,0:T(8,128)(2,1)}) %all-gather.43.cloned.1.call-update) | async-done | bytes 2097168 | tf_op jit(solution)/shard_map/all_gather | solution.py:85
  357.8 7.1 fusion.16
  364.9 4.9 reshape.283
  369.9 86.5 %reduce-scatter.15.cloned.1.call-done = f32[2,577,256]{2,1,0:T(8,128)} async-done(((f32[2,577,1024]{2,1,0:T(8,128)}), f32[2,577,256]{2,1,0:T(8,128)}) %reduce-scatter.15.cloned.1.call-update) | async-done | bytes 1181712 | tf_op jit(solution)/shard_map/reduce_scatter | solution.py:61
  458.1 17.9 %all-reduce.6 = (f32[2,577]{1,0:T(2,128)S(1)}, f32[2,577]{1,0:T(2,128)S(1)}) all-reduce(f32[2,577]{1,0:T(2,128)S(1)} %get-tuple-element.91, f32[2,577]{1,0:T(2,128)S(1)} %get-tuple-element.90), channel_id=1, replica_groups=mesh['dp'=8,'tensor'=4] {'tensor'}, use_global_device_ids=true, to_apply=%region_15.0 | all-reduce | flops 2308 | bytes 18464 | tf_op jit(solution)/shard_map/psum | solution.py:38
  478.2 11.1 all-gather.5
  489.3 37.6 %all-gather.27.cloned.1.call-done = bf16[2,577,1024]{2,1,0:T(8,128)(2,1)} async-done(((bf16[2,577,256]{2,1,0:T(8,128)(2,1)}), bf16[2,577,1024]{2,1,0:T(8,128)(2,1)}) %all-gather.27.cloned.1.call-update) | async-done | bytes 2363408 | tf_op jit(solution)/shard_map/all_gather | solution.py:57
  530.4 22.7 %all-gather.45.cloned.1.call-done = bf16[1,1024,3,256]{3,1,2,0:T(8,128)(2,1)} async-done(((bf16[1,128,3,256]{3,1,2,0:T(8,128)(2,1)}), bf16[1,1024,3,256]{3,1,2,0:T(8,128)(2,1)}) %all-gather.45.cloned.1.call-update) | async-done | bytes 1572880 | tf_op jit(solution)/shard_map/all_gather | solution.py:82
  553.2 4.1 fusion.33
  591.3 83.4 %reduce-scatter.17.cloned.1.call-done = f32[2,577,256]{2,1,0:T(8,128)} async-done(((f32[2,577,1024]{2,1,0:T(8,128)}), f32[2,577,256]{2,1,0:T(8,128)}) %reduce-scatter.17.cloned.1.call-update) | async-done | bytes 1181712 | tf_op jit(solution)/shard_map/reduce_scatter | solution.py:61
  677.1 18.6 %all-reduce.5 = (f32[2,577]{1,0:T(2,128)S(1)}, f32[2,577]{1,0:T(2,128)S(1)}) all-reduce(f32[2,577]{1,0:T(2,128)S(1)} %get-tuple-element.89, f32[2,577]{1,0:T(2,128)S(1)} %get-tuple-element.88), channel_id=1, replica_groups=mesh['dp'=8,'tensor'=4] {'tensor'}, use_global_device_ids=true, to_apply=%region_22.0 | all-reduce | flops 2308 | bytes 18464 | tf_op jit(solution)/shard_map/psum | solution.py:38
  700.1 28.4 %all-gather.31.cloned.1.call-done = bf16[2,577,1024]{2,1,0:T(8,128)(2,1)} async-done(((bf16[2,577,256]{2,1,0:T(8,128)(2,1)}), bf16[2,577,1024]{2,1,0:T(8,128)(2,1)}) %all-gather.31.cloned.1.call-update) | async-done | bytes 2363408 | tf_op jit(solution)/shard_map/all_gather | solution.py:65
  732.0 47.8 %all-gather.29.cloned.1.call-done = bf16[2,577,1024]{2,1,0:T(8,128)(2,1)} async-done(((bf16[2,577,256]{2,1,0:T(8,128)(2,1)}), bf16[2,577,1024]{2,1,0:T(8,128)(2,1)}) %all-gather.29.cloned.1.call-update) | async-done | bytes 2363408 | tf_op jit(solution)/shard_map/all_gather | solution.py:57
  779.8 3.6 reshape.285
  783.4 24.9 %all-gather.47.cloned.1.call-done = bf16[1,1024,1024]{2,1,0:T(8,128)(2,1)} async-done(((bf16[1,128,1024]{2,1,0:T(8,128)(2,1)}), bf16[1,1024,1024]{2,1,0:T(8,128)(2,1)}) %all-gather.47.cloned.1.call-update) | async-done | bytes 2097168 | tf_op jit(solution)/shard_map/all_gather | solution.py:84
  808.3 7.2 multiply_convert_fusion.2
  815.5 22.9 %all-gather.49.cloned.1.call-done = bf16[1,1024,1024]{2,1,0:T(8,128)(2,1)} async-done(((bf16[1,128,1024]{2,1,0:T(8,128)(2,1)}), bf16[1,1024,1024]{2,1,0:T(8,128)(2,1)}) %all-gather.49.cloned.1.call-update) | async-done | bytes 2097168 | tf_op jit(solution)/shard_map/all_gather | solution.py:85
  838.4 7.1 fusion.135
  847.0 4.0 convolution_convert_fusion.1
  854.6 7.2 fusion.11
  861.8 5.0 reshape.286
  866.8 36.1 %reduce-scatter.21.cloned.1.call-done = bf16[2,577,256]{2,1,0:T(8,128)(2,1)} async-done(((bf16[2,577,1024]{2,1,0:T(8,128)(2,1)}), bf16[2,577,256]{2,1,0:T(8,128)(2,1)}) %reduce-scatter.21.cloned.1.call-update) | async-done | bytes 590864 | tf_op jit(solution)/shard_map/reduce_scatter | solution.py:69
  905.2 18.0 %all-reduce.4 = (f32[2,577]{1,0:T(2,128)S(1)}, f32[2,577]{1,0:T(2,128)S(1)}) all-reduce(f32[2,577]{1,0:T(2,128)S(1)} %get-tuple-element.83, f32[2,577]{1,0:T(2,128)S(1)} %get-tuple-element.96), channel_id=1, replica_groups=mesh['dp'=8,'tensor'=4] {'tensor'}, use_global_device_ids=true, to_apply=%region_28.0 | all-reduce | flops 2308 | bytes 18464 | tf_op jit(solution)/shard_map/psum | solution.py:49
  923.2 68.0 %reduce-scatter.19.cloned.1.call-done = f32[2,577,256]{2,1,0:T(8,128)} async-done(((f32[2,577,1024]{2,1,0:T(8,128)}), f32[2,577,256]{2,1,0:T(8,128)}) %reduce-scatter.19.cloned.1.call-update) | async-done | bytes 1181712 | tf_op jit(solution)/shard_map/reduce_scatter | solution.py:61
  996.7 51.5 %all-gather.33.cloned.1.call-done = bf16[2,577,1024]{2,1,0:T(8,128)(2,1)} async-done(((bf16[2,577,256]{2,1,0:T(8,128)(2,1)}), bf16[2,577,1024]{2,1,0:T(8,128)(2,1)}) %all-gather.33.cloned.1.call-update) | async-done | bytes 2363408 | tf_op jit(solution)/shard_map/all_gather | solution.py:65
  1061.9 8.6 multiply_convert_fusion.1
  1100.6 4.9 bitcast_convert_fusion.1
  1105.5 3.6 convert_element_type.243
  1109.2 46.6 %reduce-scatter.23.cloned.1.call-done = bf16[2,577,256]{2,1,0:T(8,128)(2,1)} async-done(((bf16[2,577,1024]{2,1,0:T(8,128)(2,1)}), bf16[2,577,256]{2,1,0:T(8,128)(2,1)}) %reduce-scatter.23.cloned.1.call-update) | async-done | bytes 590864 | tf_op jit(solution)/shard_map/reduce_scatter | solution.py:69
  1157.6 17.3 %all-reduce.3 = (f32[2,577]{1,0:T(2,128)S(1)}, f32[2,577]{1,0:T(2,128)S(1)}) all-reduce(f32[2,577]{1,0:T(2,128)S(1)} %get-tuple-element.85, f32[2,577]{1,0:T(2,128)S(1)} %get-tuple-element.95), channel_id=1, replica_groups=mesh['dp'=8,'tensor'=4] {'tensor'}, use_global_device_ids=true, to_apply=%region_34.0 | all-reduce | flops 2308 | bytes 18464 | tf_op jit(solution)/shard_map/psum | solution.py:49
  1179.3 49.1 %all-gather.35.cloned.1.call-done = bf16[2,577,1024]{2,1,0:T(8,128)(2,1)} async-done(((bf16[2,577,256]{2,1,0:T(8,128)(2,1)}), bf16[2,577,1024]{2,1,0:T(8,128)(2,1)}) %all-gather.35.cloned.1.call-update) | async-done | bytes 2363408 | tf_op jit(solution)/shard_map/all_gather | solution.py:65
  1232.0 7.1 fusion.136
  1240.5 3.9 convolution_convert_fusion
  1244.4 3.6 convert_element_type.248
  1248.1 46.6 %reduce-scatter.25.cloned.1.call-done = bf16[2,577,256]{2,1,0:T(8,128)(2,1)} async-done(((bf16[2,577,1024]{2,1,0:T(8,128)(2,1)}), bf16[2,577,256]{2,1,0:T(8,128)(2,1)}) %reduce-scatter.25.cloned.1.call-update) | async-done | bytes 590864 | tf_op jit(solution)/shard_map/reduce_scatter | solution.py:69
  1297.1 17.3 %all-reduce.2 = (f32[2,577]{1,0:T(2,128)S(1)}, f32[2,577]{1,0:T(2,128)S(1)}) all-reduce(f32[2,577]{1,0:T(2,128)S(1)} %get-tuple-element.81, f32[2,577]{1,0:T(2,128)S(1)} %get-tuple-element.97), channel_id=1, replica_groups=mesh['dp'=8,'tensor'=4] {'tensor'}, use_global_device_ids=true, to_apply=%region_39.0 | all-reduce | flops 2308 | bytes 18464 | tf_op jit(solution)/shard_map/psum | solution.py:49
  1319.1 5.5 convert_bitcast_fusion.2
  1330.4 5.5 convert_bitcast_fusion
  1349.4 3.6 fusion.39
  1352.9 14.9 all-gather.37.cloned.1.call-done
  1380.3 6.8 multiply_convert_fusion
  1389.7 7.4 fusion.125
  1397.3 4.0 fusion.126
  1414.8 4.9 bitcast_convert_fusion
  1419.6 3.6 convert_element_type.256
  1432.5 42.5 %reduce-scatter.35.cloned.1.call-done = bf16[2,128,1024]{2,1,0:T(8,128)(2,1)} async-done(((bf16[2,1024,1024]{2,1,0:T(8,128)(2,1)}), bf16[2,128,1024]{2,1,0:T(8,128)(2,1)}) %reduce-scatter.35.cloned.1.call-update) | async-done | bytes 524304 | tf_op jit(solution)/shard_map/reduce_scatter | solution.py:344
  1479.8 34.9 %reduce-scatter.31.cloned.1.call-done = bf16[2,128,256]{2,1,0:T(8,128)(2,1)} async-done(((bf16[2,1024,256]{2,1,0:T(8,128)(2,1)}), bf16[2,128,256]{2,1,0:T(8,128)(2,1)}) %reduce-scatter.31.cloned.1.call-update) | async-done | bytes 131088 | tf_op jit(solution)/shard_map/reduce_scatter | solution.py:344
  1517.4 46.7 %reduce-scatter.29.cloned.1.call-done = bf16[2,128,3,256]{3,1,2,0:T(8,128)(2,1)} async-done(((bf16[2,1024,3,256]{3,1,2,0:T(8,128)(2,1)}), bf16[2,128,3,256]{3,1,2,0:T(8,128)(2,1)}) %reduce-scatter.29.cloned.1.call-update) | async-done | bytes 393232 | tf_op jit(solution)/shard_map/reduce_scatter | solution.py:344
  1568.1 46.5 %reduce-scatter.27.cloned.1.call-done = bf16[2,577,256]{2,1,0:T(8,128)(2,1)} async-done(((bf16[2,577,1024]{2,1,0:T(8,128)(2,1)}), bf16[2,577,256]{2,1,0:T(8,128)(2,1)}) %reduce-scatter.27.cloned.1.call-update) | async-done | bytes 590864 | tf_op jit(solution)/shard_map/reduce_scatter | solution.py:69
  1616.5 17.3 %all-reduce.1 = (f32[2,577]{1,0:T(2,128)S(1)}, f32[2,577]{1,0:T(2,128)S(1)}) all-reduce(f32[2,577]{1,0:T(2,128)S(1)} %get-tuple-element.87, f32[2,577]{1,0:T(2,128)S(1)} %get-tuple-element.94), channel_id=1, replica_groups=mesh['dp'=8,'tensor'=4] {'tensor'}, use_global_device_ids=true, to_apply=%region_45.0 | all-reduce | flops 2308 | bytes 18464 | tf_op jit(solution)/shard_map/psum | solution.py:49
  1637.3 22.4 %all-reduce = (f32[2,8,256]{2,1,0:T(8,128)S(1)}, f32[2,1024]{1,0:T(2,128)S(1)}) all-reduce(f32[2,8,256]{2,1,0:T(8,128)S(1)} %pad_maximum_fusion.9, f32[2,1024]{1,0:T(2,128)S(1)} %pad_maximum_fusion.11), channel_id=1, replica_groups=mesh['dp'=8,'tensor'=4] {'dp'}, use_global_device_ids=true, to_apply=%region_66.0 | all-reduce | flops 6144 | bytes 49152 | tf_op jit(solution)/shard_map/psum | solution.py:346
  (365 shorter events, 239.9 us)
Async XLA Ops:
  7.2 25.6 %copy-start.30 = (f32[2,128,3,256]{3,1,2,0:T(8,128)S(1)}, f32[2,128,3,256]{3,1,2,0:T(8,128)}, u32[]{:S(2)}) copy-start(f32[2,128,3,256]{3,1,2,0:T(8,128)} %param.18) | copy-start | bytes 2359300
  7.2 75.0 %all-gather.23.cloned.1.call-start = ((), (), s32[]{:S(2)}) async-start(), calls=%async_computation.12 | async-start | bytes 2990080 | tf_op jit(solution)/shard_map/all_gather | solution.py:57
  8.3 24.4 %copy-start.65 = (f32[1,1,256]{2,1,0:T(1,128)}, f32[1,1,256]{2,1,0:T(1,128)S(1)}, u32[]{:S(2)}) copy-start(f32[1,1,256]{2,1,0:T(1,128)S(1)} %get-tuple-element.194) | copy-start | bytes 3076
  9.8 24.1 %copy-start.43 = (f32[2,128,256]{2,1,0:T(8,128)S(1)}, f32[2,128,256]{2,1,0:T(8,128)}, u32[]{:S(2)}) copy-start(f32[2,128,256]{2,1,0:T(8,128)} %param.19) | copy-start | bytes 786436
  32.7 75.7 %all-gather.39.cloned.1.call-start = ((), (), s32[]{:S(2)}) async-start(), calls=%async_computation.32 | async-start | bytes 1769472 | tf_op jit(solution)/shard_map/all_gather | solution.py:82
  33.6 195.1 %reduce-scatter.13.cloned.1.call-start = ((), (), s32[]{:S(2)}) async-start(), calls=%async_computation.13 | async-start | bytes 5980160 | tf_op jit(solution)/shard_map/reduce_scatter | solution.py:61
  33.8 94.7 %copy-start.56 = (f32[4,64]{1,0:T(4,128)}, f32[4,64]{1,0:T(4,128)S(1)}, u32[]{:S(2)}) copy-start(f32[4,64]{1,0:T(4,128)S(1)} %add.365) | copy-start | bytes 3076
  33.9 100.7 %copy-start.58 = (f32[4,64]{1,0:T(4,128)}, f32[4,64]{1,0:T(4,128)S(1)}, u32[]{:S(2)}) copy-start(f32[4,64]{1,0:T(4,128)S(1)} %add.362) | copy-start | bytes 3076
  43.8 95.4 %copy-start.37 = (bf16[1,1024,256]{2,1,0:T(8,128)(2,1)}, bf16[1,1024,256]{2,1,0:T(8,128)(2,1)S(1)}, u32[]{:S(2)}) copy-start(bf16[1,1024,256]{2,1,0:T(8,128)(2,1)S(1)} %all-gather.1) | copy-start | bytes 1572868
  117.6 10.9 copy-start.18
  128.5 6.0 copy-start.7
  142.2 86.5 %copy-start.5 = (bf16[2,577,256]{2,0,1:T(2,128)(2,1)S(1)}, bf16[2,577,256]{2,0,1:T(2,128)(2,1)}, u32[]{:S(2)}) copy-start(bf16[2,577,256]{2,0,1:T(2,128)(2,1)} %param.15) | copy-start | bytes 1772548
  142.3 157.1 %all-gather.25.cloned.1.call-start = ((), (), s32[]{:S(2)}) async-start(), calls=%async_computation.14 | async-start | bytes 2990080 | tf_op jit(solution)/shard_map/all_gather | solution.py:57
  228.8 21.1 %copy-start.27 = (f32[2,128,1024]{2,1,0:T(8,128)S(1)}, f32[2,128,1024]{2,1,0:T(8,128)}, u32[]{:S(2)}) copy-start(f32[2,128,1024]{2,1,0:T(8,128)} %param.20) | copy-start | bytes 3145732
  249.8 77.9 %all-gather.41.cloned.1.call-start = ((), (), s32[]{:S(2)}) async-start(), calls=%async_computation.33 | async-start | bytes 2359296 | tf_op jit(solution)/shard_map/all_gather | solution.py:84
  250.8 107.0 %all-gather.43.cloned.1.call-start = ((), (), s32[]{:S(2)}) async-start(), calls=%async_computation.34 | async-start | bytes 2359296 | tf_op jit(solution)/shard_map/all_gather | solution.py:85
  253.0 203.4 %reduce-scatter.15.cloned.1.call-start = ((), (), s32[]{:S(2)}) async-start(), calls=%async_computation.15 | async-start | bytes 5980160 | tf_op jit(solution)/shard_map/reduce_scatter | solution.py:61
  369.9 157.0 %all-gather.27.cloned.1.call-start = ((), (), s32[]{:S(2)}) async-start(), calls=%async_computation.16 | async-start | bytes 2990080 | tf_op jit(solution)/shard_map/all_gather | solution.py:57
  477.3 75.9 %all-gather.45.cloned.1.call-start = ((), (), s32[]{:S(2)}) async-start(), calls=%async_computation.35 | async-start | bytes 1769472 | tf_op jit(solution)/shard_map/all_gather | solution.py:82
  478.0 196.7 %reduce-scatter.17.cloned.1.call-start = ((), (), s32[]{:S(2)}) async-start(), calls=%async_computation.17 | async-start | bytes 5980160 | tf_op jit(solution)/shard_map/reduce_scatter | solution.py:61
  562.4 12.3 copy-start.20
  588.2 140.3 %all-gather.31.cloned.1.call-start = ((), (), s32[]{:S(2)}) async-start(), calls=%async_computation.20 | async-start | bytes 2990080 | tf_op jit(solution)/shard_map/all_gather | solution.py:65
  588.9 402.3 %copy-start.68 = (f32[2]{0:T(128)}, f32[2]{0:T(128)S(1)}, u32[]{:S(2)}) copy-start(f32[2]{0:T(128)S(1)} %add_convert_fusion.15) | copy-start | bytes 28
  591.2 188.6 %all-gather.29.cloned.1.call-start = ((), (), s32[]{:S(2)}) async-start(), calls=%async_computation.18 | async-start | bytes 2990080 | tf_op jit(solution)/shard_map/all_gather | solution.py:57
  698.3 110.0 %all-gather.47.cloned.1.call-start = ((), (), s32[]{:S(2)}) async-start(), calls=%async_computation.36 | async-start | bytes 2359296 | tf_op jit(solution)/shard_map/all_gather | solution.py:84
  699.0 139.4 %all-gather.49.cloned.1.call-start = ((), (), s32[]{:S(2)}) async-start(), calls=%async_computation.37 | async-start | bytes 2359296 | tf_op jit(solution)/shard_map/all_gather | solution.py:85
  699.6 203.3 %reduce-scatter.21.cloned.1.call-start = ((), (), s32[]{:S(2)}) async-start(), calls=%async_computation.21 | async-start | bytes 2990080 | tf_op jit(solution)/shard_map/reduce_scatter | solution.py:69
  838.4 8.6 copy-start.75
  854.5 136.7 %reduce-scatter.19.cloned.1.call-start = ((), (), s32[]{:S(2)}) async-start(), calls=%async_computation.19 | async-start | bytes 5980160 | tf_op jit(solution)/shard_map/reduce_scatter | solution.py:61
  866.8 181.4 %all-gather.33.cloned.1.call-start = ((), (), s32[]{:S(2)}) async-start(), calls=%async_computation.22 | async-start | bytes 2990080 | tf_op jit(solution)/shard_map/all_gather | solution.py:65
  996.6 159.1 %reduce-scatter.23.cloned.1.call-start = ((), (), s32[]{:S(2)}) async-start(), calls=%async_computation.23 | async-start | bytes 2990080 | tf_op jit(solution)/shard_map/reduce_scatter | solution.py:69
  1061.9 8.6 copy-start.21
  1061.9 13.4 slice-start
  1061.9 13.4 slice-start.1
  1109.2 119.3 %all-gather.35.cloned.1.call-start = ((), (), s32[]{:S(2)}) async-start(), calls=%async_computation.24 | async-start | bytes 2990080 | tf_op jit(solution)/shard_map/all_gather | solution.py:65
  1179.3 115.4 %reduce-scatter.25.cloned.1.call-start = ((), (), s32[]{:S(2)}) async-start(), calls=%async_computation.25 | async-start | bytes 2990080 | tf_op jit(solution)/shard_map/reduce_scatter | solution.py:69
  1232.0 8.6 copy-start.74
  1248.0 66.3 %copy-start.16 = (f32[2,577,256]{2,1,0:T(8,128)S(1)}, f32[2,577,256]{2,1,0:T(8,128)}, u32[]{:S(2)}) copy-start(f32[2,577,256]{2,1,0:T(8,128)} %copy-done.15) | copy-start | bytes 3545092
  1248.1 119.7 %all-gather.37.cloned.1.call-start = ((), (), s32[]{:S(2)}) async-start(), calls=%async_computation.26 | async-start | bytes 2990080 | tf_op jit(solution)/shard_map/all_gather | solution.py:65
  1318.7 107.7 %reduce-scatter.33.cloned.1.call-start = ((), (), s32[]{:S(2)}) async-start(), calls=%async_computation.30 | async-start | bytes 4718592 | tf_op jit(solution)/shard_map/reduce_scatter | solution.py:344
  1330.3 144.7 %reduce-scatter.35.cloned.1.call-start = ((), (), s32[]{:S(2)}) async-start(), calls=%async_computation.31 | async-start | bytes 4718592 | tf_op jit(solution)/shard_map/reduce_scatter | solution.py:344
  1341.6 173.1 %reduce-scatter.31.cloned.1.call-start = ((), (), s32[]{:S(2)}) async-start(), calls=%async_computation.29 | async-start | bytes 1179648 | tf_op jit(solution)/shard_map/reduce_scatter | solution.py:344
  1352.9 18.4 %copy-start.38 = (bf16[1,1024,256]{2,1,0:T(8,128)(2,1)S(1)}, bf16[1,1024,256]{2,1,0:T(8,128)(2,1)}, u32[]{:S(2)}) copy-start(bf16[1,1024,256]{2,1,0:T(8,128)(2,1)} %copy-done.37) | copy-start | bytes 1572868
  1380.3 6.9 copy-start.10
  1380.3 6.9 copy-start.57
  1389.7 7.5 copy-start.19
  1397.2 166.9 %reduce-scatter.29.cloned.1.call-start = ((), (), s32[]{:S(2)}) async-start(), calls=%async_computation.28 | async-start | bytes 3538944 | tf_op jit(solution)/shard_map/reduce_scatter | solution.py:344
  1413.3 201.3 %reduce-scatter.27.cloned.1.call-start = ((), (), s32[]{:S(2)}) async-start(), calls=%async_computation.27 | async-start | bytes 2990080 | tf_op jit(solution)/shard_map/reduce_scatter | solution.py:69
  1431.1 43.9 %copy-start.24 = (f32[2,2,128,1024]{3,2,1,0:T(8,128)S(1)}, f32[2,2,128,1024]{3,2,1,0:T(8,128)}, u32[]{:S(2)}) copy-start(f32[2,2,128,1024]{3,2,1,0:T(8,128)} %param.27) | copy-start | bytes 6291460
  1478.2 36.5 %copy-start.41 = (f32[2,2,128,256]{3,2,1,0:T(8,128)S(1)}, f32[2,2,128,256]{3,2,1,0:T(8,128)}, u32[]{:S(2)}) copy-start(f32[2,2,128,256]{3,2,1,0:T(8,128)} %param.25) | copy-start | bytes 1572868
  1478.2 37.4 %copy-start.44 = (f32[2,128,256]{2,1,0:T(8,128)S(1)}, f32[2,128,256]{2,1,0:T(8,128)}, u32[]{:S(2)}) copy-start(f32[2,128,256]{2,1,0:T(8,128)} %param.19) | copy-start | bytes 786436
  1479.6 84.5 %copy-start.29 = (f32[2,2,128,3,256]{4,2,3,1,0:T(8,128)S(1)}, f32[2,2,128,3,256]{4,2,3,1,0:T(8,128)}, u32[]{:S(2)}) copy-start(f32[2,2,128,3,256]{4,2,3,1,0:T(8,128)} %param.24) | copy-start | bytes 4718596
  1515.6 49.6 %copy-start.42 = (f32[2,128,256]{2,1,0:T(8,128)}, f32[2,128,256]{2,1,0:T(8,128)S(1)}, u32[]{:S(2)}) copy-start(f32[2,128,256]{2,1,0:T(8,128)S(1)} %get-tuple-element.131) | copy-start | bytes 786436
  1516.5 48.7 %copy-start.31 = (f32[2,128,3,256]{3,1,2,0:T(8,128)S(1)}, f32[2,128,3,256]{3,1,2,0:T(8,128)}, u32[]{:S(2)}) copy-start(f32[2,128,3,256]{3,1,2,0:T(8,128)} %param.18) | copy-start | bytes 2359300
  1566.8 47.8 %copy-start.6 = (bf16[2,577,256]{2,0,1:T(2,128)(2,1)S(1)}, bf16[2,577,256]{2,0,1:T(2,128)(2,1)}, u32[]{:S(2)}) copy-start(bf16[2,577,256]{2,0,1:T(2,128)(2,1)} %param.15) | copy-start | bytes 1772548
  1566.8 47.8 %copy-start.52 = (f32[2,577]{1,0:T(2,128)S(1)}, f32[2,577]{1,0:T(2,128)}, u32[]{:S(2)}) copy-start(f32[2,577]{1,0:T(2,128)} %copy-done.51) | copy-start | bytes 13852
  1566.8 47.8 %copy-start.54 = (f32[2,577]{1,0:T(2,128)S(1)}, f32[2,577]{1,0:T(2,128)}, u32[]{:S(2)}) copy-start(f32[2,577]{1,0:T(2,128)} %copy-done.53) | copy-start | bytes 13852
  1566.8 47.8 %copy-start.66 = (f32[1,1,256]{2,1,0:T(1,128)S(1)}, f32[1,1,256]{2,1,0:T(1,128)}, u32[]{:S(2)}) copy-start(f32[1,1,256]{2,1,0:T(1,128)} %copy-done.65) | copy-start | bytes 3076
  1566.8 67.0 %copy-start.14 = (f32[2,577,256]{2,1,0:T(8,128)S(1)}, f32[2,577,256]{2,1,0:T(8,128)}, u32[]{:S(2)}) copy-start(f32[2,577,256]{2,1,0:T(8,128)} %copy-done.13) | copy-start | bytes 3545092
  1566.8 67.0 %copy-start.69 = (f32[2]{0:T(128)S(1)}, f32[2]{0:T(128)}, u32[]{:S(2)}) copy-start(f32[2]{0:T(128)} %copy-done.68) | copy-start | bytes 28
  1635.6 24.1 %copy-start.55 = (f32[2,8,256]{2,1,0:T(8,128)S(1)}, f32[2,8,256]{2,1,0:T(8,128)}, u32[]{:S(2)}) copy-start(f32[2,8,256]{2,1,0:T(8,128)} %param.22) | copy-start | bytes 49156
  1635.6 24.1 %copy-start.60 = (f32[2,2,8,256]{3,2,1,0:T(8,128)S(1)}, f32[2,2,8,256]{3,2,1,0:T(8,128)}, u32[]{:S(2)}) copy-start(f32[2,2,8,256]{3,2,1,0:T(8,128)} %param.28) | copy-start | bytes 98308
  1635.6 24.8 %copy-start.62 = (f32[2,1024]{1,0:T(2,128)S(1)}, f32[2,1024]{1,0:T(2,128)}, u32[]{:S(2)}) copy-start(f32[2,1024]{1,0:T(2,128)} %param.23) | copy-start | bytes 24580
  1635.7 24.7 %copy-start.63 = (f32[2,2,1024]{2,1,0:T(2,128)S(1)}, f32[2,2,1024]{2,1,0:T(2,128)}, u32[]{:S(2)}) copy-start(f32[2,2,1024]{2,1,0:T(2,128)} %param.29) | copy-start | bytes 49156
  (46 other events, 123.9 us)
Sparse Core Ops, SparseCore 0:
  32.8 49.2 all-gather.22
  84.6 23.7 all-gather.38
  142.4 86.3 reduce-scatter.12
  249.9 49.3 all-gather.24
  301.7 25.9 all-gather.40
  330.0 27.7 all-gather.42
  370.0 86.3 reduce-scatter.14
  477.4 49.4 all-gather.26
  529.4 23.7 all-gather.44
  588.3 86.3 reduce-scatter.16
  676.8 51.6 all-gather.30
  730.5 49.3 all-gather.28
  782.3 25.9 all-gather.46
  810.6 27.7 all-gather.48
  854.6 48.2 reduce-scatter.20
  905.1 86.0 reduce-scatter.18
  996.8 51.4 all-gather.32
  1109.3 46.4 reduce-scatter.22
  1179.4 48.9 all-gather.34
  1248.2 46.4 reduce-scatter.24
  1318.8 48.9 all-gather.36
  1371.2 49.2 reduce-scatter.32
  1423.8 51.1 reduce-scatter.34
  1478.6 35.9 reduce-scatter.30
  1518.0 46.0 reduce-scatter.28
  1566.3 48.2 reduce-scatter.26
where the time goes:
time: 1680 us; the launch traced here: 1670 us
  waiting for transfers between devices  1080 us (64%)
  blocking collectives  188 us (11%)
  matrix products  160 us (10%)
  local copies, waits for them, and re-layouts  148 us (9%)
  other arithmetic  72.7 us (4%)
    reduce_scatter x4, waiting for transfers between devices, sum_branch(): lax.psum_scatter(partial_rows, 'tensor', scatter_dimension=2, tiled=True)  324 us
    reduce_scatter x4, waiting for transfers between devices, sum_inputs(): lax.psum_scatter(partial_rows.astype(jnp.bfloat16), 'tensor', scatter_dim...  176 us
    all_gather x4, waiting for transfers between devices, share_features(): return lax.all_gather(local_rows, 'tensor', axis=2, tiled=True)  170 us
    all_gather x4, waiting for transfers between devices, share_grads(): return lax.all_gather(local_rows, 'tensor', axis=2, tiled=True)  144 us
    reduce_scatter x4, waiting for transfers between devices, on_device(): lax.psum_scatter(as_sent(stacked), 'dp', scatter_dimension=1, tiled=True)  124 us
    psum x4, blocking collectives, layer_statistics(): lax.psum((jnp.sum(hidden_state, -1), jnp.sum(hidden_state * hidden_state,...  75.1 us
    psum x4, blocking collectives, norm_back(): lax.psum((jnp.sum(d_hat, -1), jnp.sum(d_hat * normed, -1)), 'tensor')  69.8 us
    all_gather x2, waiting for transfers between devices, fetch_weights(): lax.all_gather(pieces[2], 'dp', axis=0, tiled=True)  49.6 us
  transfers between devices with their start and end apart: 26, of which 25 were waited for; matrix products, arithmetic and copies ran while one was open for 10% of the time, Pallas kernels for 0%

commit v1 on v0

--- a/solution.py
+++ b/solution.py
@@ -54,7 +54,9 @@
 
 
 def share_features(local_rows):
-    return lax.all_gather(local_rows, "tensor", axis=2, tiled=True)
+    return jnp.concatenate(
+        lax.all_to_all(jnp.stack([local_rows] * lax.axis_size("tensor")), "tensor", 0, 0), axis=2
+    )
 
 
 def sum_branch(partial_rows):

time: 1680 us -> 1610 us (0.958)
  waiting for transfers between devices: 1080 us -> 966 us
  local copies, waits for them, and re-layouts: 148 us -> 179 us
  starting transfers between devices: 2.52 us -> 24.2 us
    all_gather x4 -> x0, waiting for transfers between devices: 170 us -> none  [share_features(): return lax.all_gather(local_rows, 'tensor', axis=2, tiled=True)]
    all_to_all x0 -> x4, waiting for transfers between devices: none -> 148 us  [share_features(): lax.all_to_all(jnp.stack([local_rows] * lax.axis_size('tensor')), 'tensor...]
    all_gather x2, waiting for transfers between devices: 45.5 us -> 0.01 us  [fetch_weights(): lax.all_gather(pieces[0], 'dp', axis=0, tiled=True)]
    all_gather x2, waiting for transfers between devices: 49.6 us -> 13.7 us  [fetch_weights(): lax.all_gather(pieces[2], 'dp', axis=0, tiled=True)]
    all_gather x2, waiting for transfers between devices: 45.9 us -> 22.9 us  [fetch_weights(): lax.all_gather(pieces[3], 'dp', axis=0, tiled=True)]
    all_to_all x0 -> x4, starting transfers between devices: none -> 22.6 us  [share_features(): lax.all_to_all(jnp.stack([local_rows] * lax.axis_size('tensor')), 'tensor...]
    another operation x0 -> x6, local copies, waits for them, and re-layouts: none -> 21.4 us  [the longest x2 10.9 us: on_device(): first_normalized = share_features((first_centered_scaled * vector_rows[0]...]
    all_gather x4, waiting for transfers between devices: 144 us -> 161 us  [share_grads(): return lax.all_gather(local_rows, 'tensor', axis=2, tiled=True)]
  transfers between devices with their start and end apart: 26 -> 26, of which waited for: 25 -> 21; matrix products, arithmetic and copies ran while one was open for 10% -> 11% of each run, Pallas kernels for 0% -> 0%
where the time goes in v1:
time: 1610 us; the launch traced here: 1600 us
  waiting for transfers between devices  966 us (60%)
  blocking collectives  188 us (12%)
  local copies, waits for them, and re-layouts  179 us (11%)
  matrix products  160 us (10%)
  other arithmetic  68.2 us (4%)
  starting transfers between devices  24.2 us (2%)
  between operations  16.5 us (1%)
    reduce_scatter x4, waiting for transfers between devices, sum_branch(): lax.psum_scatter(partial_rows, 'tensor', scatter_dimension=2, tiled=True)  319 us
    reduce_scatter x4, waiting for transfers between devices, sum_inputs(): lax.psum_scatter(partial_rows.astype(jnp.bfloat16), 'tensor', scatter_dim...  176 us
    all_gather x4, waiting for transfers between devices, share_grads(): return lax.all_gather(local_rows, 'tensor', axis=2, tiled=True)  161 us
    all_to_all x4, waiting for transfers between devices, share_features(): lax.all_to_all(jnp.stack([local_rows] * lax.axis_size('tensor')), 'tensor...  148 us
    reduce_scatter x4, waiting for transfers between devices, on_device(): lax.psum_scatter(as_sent(stacked), 'dp', scatter_dimension=1, tiled=True)  124 us
    psum x4, blocking collectives, layer_statistics(): lax.psum((jnp.sum(hidden_state, -1), jnp.sum(hidden_state * hidden_state,...  75 us
    psum x4, blocking collectives, norm_back(): lax.psum((jnp.sum(d_hat, -1), jnp.sum(d_hat * normed, -1)), 'tensor')  69.8 us
    unnamed x192, local copies, waits for them, and re-layouts  33.1 us
  transfers between devices with their start and end apart: 26, of which 21 were waited for; matrix products, arithmetic and copies ran while one was open for 11% of the time, Pallas kernels for 0%

profile of v1, /device:TPU:0, one launch (start us, length us, event | category | flops | bytes accessed | tf_op | source)
XLA Modules:
  0.0 1602.4 jit_solution(5338226936141937372)
XLA Ops:
  9.8 20.5 %all-reduce.8 = (f32[2,577]{1,0:T(2,128)S(1)}, f32[2,577]{1,0:T(2,128)S(1)}) all-reduce(f32[2,577]{1,0:T(2,128)S(1)} %get-tuple-element.143, f32[2,577]{1,0:T(2,128)S(1)} %get-tuple-element.142), channel_id=1, replica_groups=mesh['dp'=8,'tensor'=4] {'tensor'}, use_global_device_ids=true, to_apply=%region_3.0 | all-reduce | flops 2308 | bytes 18464 | tf_op jit(solution)/shard_map/psum | solution.py:38
  35.4 4.7 all-to-all-start
  41.3 9.9 all-gather.1
  51.1 39.4 %all-to-all-done = bf16[4,2,577,256]{3,1,2,0:T(2,128)(2,1)} async-done(((bf16[4,2,577,256]{3,1,2,0:T(2,128)(2,1)}), bf16[4,2,577,256]{3,1,2,0:T(2,128)(2,1)}, u32[]{:S(2)}, u32[]{:S(2)}) %all-to-all-start) | async-done | bytes 2363424 | tf_op jit(solution)/shard_map/all_to_all | solution.py:58
  90.6 4.0 copy.241
  94.6 5.4 reshape.311
  100.0 4.2 fusion.36
  120.0 3.9 multiply_reduce_fusion.1
  135.9 83.5 %reduce-scatter.13.cloned.1.call-done = f32[2,577,256]{2,1,0:T(8,128)} async-done(((f32[2,577,1024]{2,1,0:T(8,128)}), f32[2,577,256]{2,1,0:T(8,128)}) %reduce-scatter.13.cloned.1.call-update) | async-done | bytes 1181712 | tf_op jit(solution)/shard_map/reduce_scatter | solution.py:63
  221.1 18.0 %all-reduce.7 = (f32[2,577]{1,0:T(2,128)S(1)}, f32[2,577]{1,0:T(2,128)S(1)}) all-reduce(f32[2,577]{1,0:T(2,128)S(1)} %get-tuple-element.133, f32[2,577]{1,0:T(2,128)S(1)} %get-tuple-element.132), channel_id=1, replica_groups=mesh['dp'=8,'tensor'=4] {'tensor'}, use_global_device_ids=true, to_apply=%region_10.0 | all-reduce | flops 2308 | bytes 18464 | tf_op jit(solution)/shard_map/psum | solution.py:38
  243.2 4.7 all-to-all-start.1
  248.9 49.5 %all-to-all-done.1 = bf16[4,2,577,256]{3,1,2,0:T(2,128)(2,1)} async-done(((bf16[4,2,577,256]{3,1,2,0:T(2,128)(2,1)}), bf16[4,2,577,256]{3,1,2,0:T(2,128)(2,1)}, u32[]{:S(2)}, u32[]{:S(2)}) %all-to-all-start.1) | async-done | bytes 2363424 | tf_op jit(solution)/shard_map/all_to_all | solution.py:58
  304.2 7.2 multiply_convert_fusion.3
  311.4 7.1 fusion.16
  318.5 4.9 reshape.291
  323.5 85.6 %reduce-scatter.15.cloned.1.call-done = f32[2,577,256]{2,1,0:T(8,128)} async-done(((f32[2,577,1024]{2,1,0:T(8,128)}), f32[2,577,256]{2,1,0:T(8,128)}) %reduce-scatter.15.cloned.1.call-update) | async-done | bytes 1181712 | tf_op jit(solution)/shard_map/reduce_scatter | solution.py:63
  410.8 18.0 %all-reduce.6 = (f32[2,577]{1,0:T(2,128)S(1)}, f32[2,577]{1,0:T(2,128)S(1)}) all-reduce(f32[2,577]{1,0:T(2,128)S(1)} %get-tuple-element.131, f32[2,577]{1,0:T(2,128)S(1)} %get-tuple-element.130), channel_id=1, replica_groups=mesh['dp'=8,'tensor'=4] {'tensor'}, use_global_device_ids=true, to_apply=%region_15.0 | all-reduce | flops 2308 | bytes 18464 | tf_op jit(solution)/shard_map/psum | solution.py:38
  432.3 4.5 all-to-all-start.2
  437.6 11.0 all-gather.5
  448.6 38.8 %all-to-all-done.2 = bf16[4,2,577,256]{3,1,2,0:T(2,128)(2,1)} async-done(((bf16[4,2,577,256]{3,1,2,0:T(2,128)(2,1)}), bf16[4,2,577,256]{3,1,2,0:T(2,128)(2,1)}, u32[]{:S(2)}, u32[]{:S(2)}) %all-to-all-start.2) | async-done | bytes 2363424 | tf_op jit(solution)/shard_map/all_to_all | solution.py:58
  487.4 4.0 copy.253
  491.4 5.4 reshape.313
  496.9 4.1 fusion.33
  535.8 81.8 %reduce-scatter.17.cloned.1.call-done = f32[2,577,256]{2,1,0:T(8,128)} async-done(((f32[2,577,1024]{2,1,0:T(8,128)}), f32[2,577,256]{2,1,0:T(8,128)}) %reduce-scatter.17.cloned.1.call-update) | async-done | bytes 1181712 | tf_op jit(solution)/shard_map/reduce_scatter | solution.py:63
  620.0 18.6 %all-reduce.5 = (f32[2,577]{1,0:T(2,128)S(1)}, f32[2,577]{1,0:T(2,128)S(1)}) all-reduce(f32[2,577]{1,0:T(2,128)S(1)} %get-tuple-element.129, f32[2,577]{1,0:T(2,128)S(1)} %get-tuple-element.128), channel_id=1, replica_groups=mesh['dp'=8,'tensor'=4] {'tensor'}, use_global_device_ids=true, to_apply=%region_22.0 | all-reduce | flops 2308 | bytes 18464 | tf_op jit(solution)/shard_map/psum | solution.py:38
  643.4 8.8 all-to-all-start.3
  653.0 45.2 %all-gather.19.cloned.1.call-done = bf16[2,577,1024]{2,1,0:T(8,128)(2,1)} async-done(((bf16[2,577,256]{2,1,0:T(8,128)(2,1)}), bf16[2,577,1024]{2,1,0:T(8,128)(2,1)}) %all-gather.19.cloned.1.call-update) | async-done | bytes 2363408 | tf_op jit(solution)/shard_map/all_gather | solution.py:67
  701.7 20.2 %all-to-all-done.3 = bf16[4,2,577,256]{3,1,2,0:T(2,128)(2,1)} async-done(((bf16[4,2,577,256]{3,1,2,0:T(2,128)(2,1)}), bf16[4,2,577,256]{3,1,2,0:T(2,128)(2,1)}, u32[]{:S(2)}, u32[]{:S(2)}) %all-to-all-start.3) | async-done | bytes 2363424 | tf_op jit(solution)/shard_map/all_to_all | solution.py:58
  727.4 13.7 all-gather.35.cloned.1.call-done
  741.1 7.2 multiply_convert_fusion.2
  748.4 22.9 %all-gather.37.cloned.1.call-done = bf16[1,1024,1024]{2,1,0:T(8,128)(2,1)} async-done(((bf16[1,128,1024]{2,1,0:T(8,128)(2,1)}), bf16[1,1024,1024]{2,1,0:T(8,128)(2,1)}) %all-gather.37.cloned.1.call-update) | async-done | bytes 2097168 | tf_op jit(solution)/shard_map/all_gather | solution.py:87
  771.3 7.1 fusion.135
  779.8 4.0 convolution_convert_fusion.1
  787.4 7.2 fusion.11
  794.6 5.0 reshape.294
  799.7 36.1 %reduce-scatter.21.cloned.1.call-done = bf16[2,577,256]{2,1,0:T(8,128)(2,1)} async-done(((bf16[2,577,1024]{2,1,0:T(8,128)(2,1)}), bf16[2,577,256]{2,1,0:T(8,128)(2,1)}) %reduce-scatter.21.cloned.1.call-update) | async-done | bytes 590864 | tf_op jit(solution)/shard_map/reduce_scatter | solution.py:71
  838.0 18.0 %all-reduce.4 = (f32[2,577]{1,0:T(2,128)S(1)}, f32[2,577]{1,0:T(2,128)S(1)}) all-reduce(f32[2,577]{1,0:T(2,128)S(1)} %get-tuple-element.123, f32[2,577]{1,0:T(2,128)S(1)} %get-tuple-element.136), channel_id=1, replica_groups=mesh['dp'=8,'tensor'=4] {'tensor'}, use_global_device_ids=true, to_apply=%region_28.0 | all-reduce | flops 2308 | bytes 18464 | tf_op jit(solution)/shard_map/psum | solution.py:49
  856.0 68.1 %reduce-scatter.19.cloned.1.call-done = f32[2,577,256]{2,1,0:T(8,128)} async-done(((f32[2,577,1024]{2,1,0:T(8,128)}), f32[2,577,256]{2,1,0:T(8,128)}) %reduce-scatter.19.cloned.1.call-update) | async-done | bytes 1181712 | tf_op jit(solution)/shard_map/reduce_scatter | solution.py:63
  929.5 51.5 %all-gather.21.cloned.1.call-done = bf16[2,577,1024]{2,1,0:T(8,128)(2,1)} async-done(((bf16[2,577,256]{2,1,0:T(8,128)(2,1)}), bf16[2,577,1024]{2,1,0:T(8,128)(2,1)}) %all-gather.21.cloned.1.call-update) | async-done | bytes 2363408 | tf_op jit(solution)/shard_map/all_gather | solution.py:67
  994.8 8.6 multiply_convert_fusion.1
  1033.7 4.9 bitcast_convert_fusion.1
  1038.6 3.6 convert_element_type.243
  1042.3 46.6 %reduce-scatter.23.cloned.1.call-done = bf16[2,577,256]{2,1,0:T(8,128)(2,1)} async-done(((bf16[2,577,1024]{2,1,0:T(8,128)(2,1)}), bf16[2,577,256]{2,1,0:T(8,128)(2,1)}) %reduce-scatter.23.cloned.1.call-update) | async-done | bytes 590864 | tf_op jit(solution)/shard_map/reduce_scatter | solution.py:71
  1090.6 17.2 %all-reduce.3 = (f32[2,577]{1,0:T(2,128)S(1)}, f32[2,577]{1,0:T(2,128)S(1)}) all-reduce(f32[2,577]{1,0:T(2,128)S(1)} %get-tuple-element.125, f32[2,577]{1,0:T(2,128)S(1)} %get-tuple-element.135), channel_id=1, replica_groups=mesh['dp'=8,'tensor'=4] {'tensor'}, use_global_device_ids=true, to_apply=%region_34.0 | all-reduce | flops 2308 | bytes 18464 | tf_op jit(solution)/shard_map/psum | solution.py:49
  1112.4 49.1 %all-gather.23.cloned.1.call-done = bf16[2,577,1024]{2,1,0:T(8,128)(2,1)} async-done(((bf16[2,577,256]{2,1,0:T(8,128)(2,1)}), bf16[2,577,1024]{2,1,0:T(8,128)(2,1)}) %all-gather.23.cloned.1.call-update) | async-done | bytes 2363408 | tf_op jit(solution)/shard_map/all_gather | solution.py:67
  1165.1 7.1 fusion.136
  1173.6 3.9 convolution_convert_fusion
  1177.6 3.6 convert_element_type.248
  1181.2 46.6 %reduce-scatter.25.cloned.1.call-done = bf16[2,577,256]{2,1,0:T(8,128)(2,1)} async-done(((bf16[2,577,1024]{2,1,0:T(8,128)(2,1)}), bf16[2,577,256]{2,1,0:T(8,128)(2,1)}) %reduce-scatter.25.cloned.1.call-update) | async-done | bytes 590864 | tf_op jit(solution)/shard_map/reduce_scatter | solution.py:71
  1230.2 17.2 %all-reduce.2 = (f32[2,577]{1,0:T(2,128)S(1)}, f32[2,577]{1,0:T(2,128)S(1)}) all-reduce(f32[2,577]{1,0:T(2,128)S(1)} %get-tuple-element.121, f32[2,577]{1,0:T(2,128)S(1)} %get-tuple-element.137), channel_id=1, replica_groups=mesh['dp'=8,'tensor'=4] {'tensor'}, use_global_device_ids=true, to_apply=%region_39.0 | all-reduce | flops 2308 | bytes 18464 | tf_op jit(solution)/shard_map/psum | solution.py:49
  1252.0 5.5 convert_bitcast_fusion.2
  1263.3 5.5 convert_bitcast_fusion
  1285.8 15.1 all-gather.25.cloned.1.call-done
  1313.5 6.8 multiply_convert_fusion
  1322.9 7.4 fusion.125
  1330.4 4.0 fusion.126
  1348.1 4.9 bitcast_convert_fusion
  1352.9 3.6 convert_element_type.256
  1365.9 42.0 %reduce-scatter.35.cloned.1.call-done = bf16[2,128,1024]{2,1,0:T(8,128)(2,1)} async-done(((bf16[2,1024,1024]{2,1,0:T(8,128)(2,1)}), bf16[2,128,1024]{2,1,0:T(8,128)(2,1)}) %reduce-scatter.35.cloned.1.call-update) | async-done | bytes 524304 | tf_op jit(solution)/shard_map/reduce_scatter | solution.py:346
  1412.7 34.8 %reduce-scatter.31.cloned.1.call-done = bf16[2,128,256]{2,1,0:T(8,128)(2,1)} async-done(((bf16[2,1024,256]{2,1,0:T(8,128)(2,1)}), bf16[2,128,256]{2,1,0:T(8,128)(2,1)}) %reduce-scatter.31.cloned.1.call-update) | async-done | bytes 131088 | tf_op jit(solution)/shard_map/reduce_scatter | solution.py:346
  1450.3 46.7 %reduce-scatter.29.cloned.1.call-done = bf16[2,128,3,256]{3,1,2,0:T(8,128)(2,1)} async-done(((bf16[2,1024,3,256]{3,1,2,0:T(8,128)(2,1)}), bf16[2,128,3,256]{3,1,2,0:T(8,128)(2,1)}) %reduce-scatter.29.cloned.1.call-update) | async-done | bytes 393232 | tf_op jit(solution)/shard_map/reduce_scatter | solution.py:346
  1501.0 46.6 %reduce-scatter.27.cloned.1.call-done = bf16[2,577,256]{2,1,0:T(8,128)(2,1)} async-done(((bf16[2,577,1024]{2,1,0:T(8,128)(2,1)}), bf16[2,577,256]{2,1,0:T(8,128)(2,1)}) %reduce-scatter.27.cloned.1.call-update) | async-done | bytes 590864 | tf_op jit(solution)/shard_map/reduce_scatter | solution.py:71
  1549.5 17.3 %all-reduce.1 = (f32[2,577]{1,0:T(2,128)S(1)}, f32[2,577]{1,0:T(2,128)S(1)}) all-reduce(f32[2,577]{1,0:T(2,128)S(1)} %get-tuple-element.127, f32[2,577]{1,0:T(2,128)S(1)} %get-tuple-element.134), channel_id=1, replica_groups=mesh['dp'=8,'tensor'=4] {'tensor'}, use_global_device_ids=true, to_apply=%region_45.0 | all-reduce | flops 2308 | bytes 18464 | tf_op jit(solution)/shard_map/psum | solution.py:49
  1570.4 22.4 %all-reduce = (f32[2,8,256]{2,1,0:T(8,128)S(1)}, f32[2,1024]{1,0:T(2,128)S(1)}) all-reduce(f32[2,8,256]{2,1,0:T(8,128)S(1)} %pad_maximum_fusion.9, f32[2,1024]{1,0:T(2,128)S(1)} %pad_maximum_fusion.11), channel_id=1, replica_groups=mesh['dp'=8,'tensor'=4] {'dp'}, use_global_device_ids=true, to_apply=%region_66.0 | all-reduce | flops 6144 | bytes 49152 | tf_op jit(solution)/shard_map/psum | solution.py:348
  (389 shorter events, 261.0 us)
Async XLA Ops:
  8.3 27.2 %copy-start.72 = (f32[1,1,256]{2,1,0:T(1,128)}, f32[1,1,256]{2,1,0:T(1,128)S(1)}, u32[]{:S(2)}) copy-start(f32[1,1,256]{2,1,0:T(1,128)S(1)} %get-tuple-element.234) | copy-start | bytes 3076
  8.3 230.9 %copy-start.68 = (f32[1,1,256]{2,1,0:T(1,128)}, f32[1,1,256]{2,1,0:T(1,128)S(1)}, u32[]{:S(2)}) copy-start(f32[1,1,256]{2,1,0:T(1,128)S(1)} %get-tuple-element.229) | copy-start | bytes 3076
  35.4 55.1 %all-to-all-start = ((bf16[4,2,577,256]{3,1,2,0:T(2,128)(2,1)}), bf16[4,2,577,256]{3,1,2,0:T(2,128)(2,1)}, u32[]{:S(2)}, u32[]{:S(2)}) async-start(bf16[4,2,577,256]{3,1,2,0:T(2,128)(2,1)} %stack.217), calls=%async_computation | async-start | bytes 4726784 | tf_op jit(solution)/shard_map/all_to_all | solution.py:58
  40.1 59.9 %all-gather.27.cloned.1.call-start = ((), (), s32[]{:S(2)}) async-start(), calls=%async_computation.32 | async-start | bytes 1769472 | tf_op jit(solution)/shard_map/all_gather | solution.py:84
  41.0 178.4 %reduce-scatter.13.cloned.1.call-start = ((), (), s32[]{:S(2)}) async-start(), calls=%async_computation.16 | async-start | bytes 5980160 | tf_op jit(solution)/shard_map/reduce_scatter | solution.py:63
  41.1 78.9 %copy-start.61 = (f32[4,64]{1,0:T(4,128)}, f32[4,64]{1,0:T(4,128)S(1)}, u32[]{:S(2)}) copy-start(f32[4,64]{1,0:T(4,128)S(1)} %add.365) | copy-start | bytes 3076
  41.2 84.8 %copy-start.63 = (f32[4,64]{1,0:T(4,128)}, f32[4,64]{1,0:T(4,128)S(1)}, u32[]{:S(2)}) copy-start(f32[4,64]{1,0:T(4,128)S(1)} %add.362) | copy-start | bytes 3076
  51.1 79.6 %copy-start.38 = (bf16[1,1024,256]{2,1,0:T(8,128)(2,1)}, bf16[1,1024,256]{2,1,0:T(8,128)(2,1)S(1)}, u32[]{:S(2)}) copy-start(bf16[1,1024,256]{2,1,0:T(8,128)(2,1)S(1)} %all-gather.1) | copy-start | bytes 1572868
  108.7 11.3 copy-start.18
  133.8 85.6 %copy-start.5 = (bf16[2,577,256]{2,0,1:T(2,128)(2,1)S(1)}, bf16[2,577,256]{2,0,1:T(2,128)(2,1)}, u32[]{:S(2)}) copy-start(bf16[2,577,256]{2,0,1:T(2,128)(2,1)} %param.15) | copy-start | bytes 1772548
  133.8 170.4 %all-gather.29.cloned.1.call-start = ((), (), s32[]{:S(2)}) async-start(), calls=%async_computation.33 | async-start | bytes 2359296 | tf_op jit(solution)/shard_map/all_gather | solution.py:86
  243.2 55.3 %all-to-all-start.1 = ((bf16[4,2,577,256]{3,1,2,0:T(2,128)(2,1)}), bf16[4,2,577,256]{3,1,2,0:T(2,128)(2,1)}, u32[]{:S(2)}, u32[]{:S(2)}) async-start(bf16[4,2,577,256]{3,1,2,0:T(2,128)(2,1)} %stack.218), calls=%async_computation.2 | async-start | bytes 4726784 | tf_op jit(solution)/shard_map/all_to_all | solution.py:58
  247.9 63.5 %all-gather.31.cloned.1.call-start = ((), (), s32[]{:S(2)}) async-start(), calls=%async_computation.34 | async-start | bytes 2359296 | tf_op jit(solution)/shard_map/all_gather | solution.py:87
  248.8 160.2 %reduce-scatter.15.cloned.1.call-start = ((), (), s32[]{:S(2)}) async-start(), calls=%async_computation.17 | async-start | bytes 5980160 | tf_op jit(solution)/shard_map/reduce_scatter | solution.py:63
  432.3 55.1 %all-to-all-start.2 = ((bf16[4,2,577,256]{3,1,2,0:T(2,128)(2,1)}), bf16[4,2,577,256]{3,1,2,0:T(2,128)(2,1)}, u32[]{:S(2)}, u32[]{:S(2)}) async-start(bf16[4,2,577,256]{3,1,2,0:T(2,128)(2,1)} %stack.219), calls=%async_computation.4 | async-start | bytes 4726784 | tf_op jit(solution)/shard_map/all_to_all | solution.py:58
  436.8 60.1 %all-gather.33.cloned.1.call-start = ((), (), s32[]{:S(2)}) async-start(), calls=%async_computation.35 | async-start | bytes 1769472 | tf_op jit(solution)/shard_map/all_gather | solution.py:84
  437.4 180.3 %reduce-scatter.17.cloned.1.call-start = ((), (), s32[]{:S(2)}) async-start(), calls=%async_computation.18 | async-start | bytes 5980160 | tf_op jit(solution)/shard_map/reduce_scatter | solution.py:63
  505.9 12.7 copy-start.20
  532.1 166.2 %all-gather.19.cloned.1.call-start = ((), (), s32[]{:S(2)}) async-start(), calls=%async_computation.20 | async-start | bytes 2990080 | tf_op jit(solution)/shard_map/all_gather | solution.py:67
  532.8 391.3 %copy-start.75 = (f32[2]{0:T(128)}, f32[2]{0:T(128)S(1)}, u32[]{:S(2)}) copy-start(f32[2]{0:T(128)S(1)} %add_convert_fusion.15) | copy-start | bytes 28
  535.1 206.0 %all-gather.35.cloned.1.call-start = ((), (), s32[]{:S(2)}) async-start(), calls=%async_computation.36 | async-start | bytes 2359296 | tf_op jit(solution)/shard_map/all_gather | solution.py:86
  643.4 78.5 %all-to-all-start.3 = ((bf16[4,2,577,256]{3,1,2,0:T(2,128)(2,1)}), bf16[4,2,577,256]{3,1,2,0:T(2,128)(2,1)}, u32[]{:S(2)}, u32[]{:S(2)}) async-start(bf16[4,2,577,256]{3,1,2,0:T(2,128)(2,1)} %stack.220), calls=%async_computation.6 | async-start | bytes 4726784 | tf_op jit(solution)/shard_map/all_to_all | solution.py:58
  652.2 119.0 %all-gather.37.cloned.1.call-start = ((), (), s32[]{:S(2)}) async-start(), calls=%async_computation.37 | async-start | bytes 2359296 | tf_op jit(solution)/shard_map/all_gather | solution.py:87
  652.8 183.0 %reduce-scatter.21.cloned.1.call-start = ((), (), s32[]{:S(2)}) async-start(), calls=%async_computation.21 | async-start | bytes 2990080 | tf_op jit(solution)/shard_map/reduce_scatter | solution.py:71
  771.3 8.6 copy-start.82
  787.4 136.7 %reduce-scatter.19.cloned.1.call-start = ((), (), s32[]{:S(2)}) async-start(), calls=%async_computation.19 | async-start | bytes 5980160 | tf_op jit(solution)/shard_map/reduce_scatter | solution.py:63
  799.6 181.4 %all-gather.21.cloned.1.call-start = ((), (), s32[]{:S(2)}) async-start(), calls=%async_computation.22 | async-start | bytes 2990080 | tf_op jit(solution)/shard_map/all_gather | solution.py:67
  929.5 159.4 %reduce-scatter.23.cloned.1.call-start = ((), (), s32[]{:S(2)}) async-start(), calls=%async_computation.23 | async-start | bytes 2990080 | tf_op jit(solution)/shard_map/reduce_scatter | solution.py:71
  994.8 8.6 copy-start.21
  994.8 13.4 slice-start
  994.8 13.4 slice-start.1
  1042.2 119.3 %all-gather.23.cloned.1.call-start = ((), (), s32[]{:S(2)}) async-start(), calls=%async_computation.24 | async-start | bytes 2990080 | tf_op jit(solution)/shard_map/all_gather | solution.py:67
  1112.3 115.5 %reduce-scatter.25.cloned.1.call-start = ((), (), s32[]{:S(2)}) async-start(), calls=%async_computation.25 | async-start | bytes 2990080 | tf_op jit(solution)/shard_map/reduce_scatter | solution.py:71
  1165.0 8.6 copy-start.81
  1181.2 46.7 %copy-start.53 = (f32[2,577]{1,0:T(2,128)S(1)}, f32[2,577]{1,0:T(2,128)}, u32[]{:S(2)}) copy-start(f32[2,577]{1,0:T(2,128)} %copy-done.52) | copy-start | bytes 13852
  1181.2 46.7 %copy-start.55 = (f32[2,577]{1,0:T(2,128)S(1)}, f32[2,577]{1,0:T(2,128)}, u32[]{:S(2)}) copy-start(f32[2,577]{1,0:T(2,128)} %copy-done.54) | copy-start | bytes 13852
  1181.2 46.7 %copy-start.69 = (f32[1,1,256]{2,1,0:T(1,128)S(1)}, f32[1,1,256]{2,1,0:T(1,128)}, u32[]{:S(2)}) copy-start(f32[1,1,256]{2,1,0:T(1,128)} %copy-done.68) | copy-start | bytes 3076
  1181.2 66.3 %copy-start.16 = (f32[2,577,256]{2,1,0:T(8,128)S(1)}, f32[2,577,256]{2,1,0:T(8,128)}, u32[]{:S(2)}) copy-start(f32[2,577,256]{2,1,0:T(8,128)} %copy-done.15) | copy-start | bytes 3545092
  1181.2 119.7 %all-gather.25.cloned.1.call-start = ((), (), s32[]{:S(2)}) async-start(), calls=%async_computation.26 | async-start | bytes 2990080 | tf_op jit(solution)/shard_map/all_gather | solution.py:67
  1251.8 107.9 %reduce-scatter.33.cloned.1.call-start = ((), (), s32[]{:S(2)}) async-start(), calls=%async_computation.30 | async-start | bytes 4718592 | tf_op jit(solution)/shard_map/reduce_scatter | solution.py:346
  1263.2 144.8 %reduce-scatter.35.cloned.1.call-start = ((), (), s32[]{:S(2)}) async-start(), calls=%async_computation.31 | async-start | bytes 4718592 | tf_op jit(solution)/shard_map/reduce_scatter | solution.py:346
  1274.4 173.2 %reduce-scatter.31.cloned.1.call-start = ((), (), s32[]{:S(2)}) async-start(), calls=%async_computation.29 | async-start | bytes 1179648 | tf_op jit(solution)/shard_map/reduce_scatter | solution.py:346
  1285.8 18.7 %copy-start.39 = (bf16[1,1024,256]{2,1,0:T(8,128)(2,1)S(1)}, bf16[1,1024,256]{2,1,0:T(8,128)(2,1)}, u32[]{:S(2)}) copy-start(bf16[1,1024,256]{2,1,0:T(8,128)(2,1)} %copy-done.38) | copy-start | bytes 1572868
  1313.5 6.8 copy-start.10
  1313.5 6.8 copy-start.62
  1322.9 7.5 copy-start.19
  1330.3 166.7 %reduce-scatter.29.cloned.1.call-start = ((), (), s32[]{:S(2)}) async-start(), calls=%async_computation.28 | async-start | bytes 3538944 | tf_op jit(solution)/shard_map/reduce_scatter | solution.py:346
  1346.6 201.0 %reduce-scatter.27.cloned.1.call-start = ((), (), s32[]{:S(2)}) async-start(), calls=%async_computation.27 | async-start | bytes 2990080 | tf_op jit(solution)/shard_map/reduce_scatter | solution.py:71
  1364.5 43.5 %copy-start.24 = (f32[2,2,128,1024]{3,2,1,0:T(8,128)S(1)}, f32[2,2,128,1024]{3,2,1,0:T(8,128)}, u32[]{:S(2)}) copy-start(f32[2,2,128,1024]{3,2,1,0:T(8,128)} %param.27) | copy-start | bytes 6291460
  1411.1 36.5 %copy-start.42 = (f32[2,2,128,256]{3,2,1,0:T(8,128)S(1)}, f32[2,2,128,256]{3,2,1,0:T(8,128)}, u32[]{:S(2)}) copy-start(f32[2,2,128,256]{3,2,1,0:T(8,128)} %param.25) | copy-start | bytes 1572868
  1411.1 37.4 %copy-start.45 = (f32[2,128,256]{2,1,0:T(8,128)S(1)}, f32[2,128,256]{2,1,0:T(8,128)}, u32[]{:S(2)}) copy-start(f32[2,128,256]{2,1,0:T(8,128)} %param.19) | copy-start | bytes 786436
  1412.6 84.5 %copy-start.30 = (f32[2,2,128,3,256]{4,2,3,1,0:T(8,128)S(1)}, f32[2,2,128,3,256]{4,2,3,1,0:T(8,128)}, u32[]{:S(2)}) copy-start(f32[2,2,128,3,256]{4,2,3,1,0:T(8,128)} %param.24) | copy-start | bytes 4718596
  1448.5 49.7 %copy-start.43 = (f32[2,128,256]{2,1,0:T(8,128)}, f32[2,128,256]{2,1,0:T(8,128)S(1)}, u32[]{:S(2)}) copy-start(f32[2,128,256]{2,1,0:T(8,128)S(1)} %get-tuple-element.171) | copy-start | bytes 786436
  1449.5 48.7 %copy-start.32 = (f32[2,128,3,256]{3,1,2,0:T(8,128)S(1)}, f32[2,128,3,256]{3,1,2,0:T(8,128)}, u32[]{:S(2)}) copy-start(f32[2,128,3,256]{3,1,2,0:T(8,128)} %param.18) | copy-start | bytes 2359300
  1499.7 47.9 %copy-start.6 = (bf16[2,577,256]{2,0,1:T(2,128)(2,1)S(1)}, bf16[2,577,256]{2,0,1:T(2,128)(2,1)}, u32[]{:S(2)}) copy-start(bf16[2,577,256]{2,0,1:T(2,128)(2,1)} %param.15) | copy-start | bytes 1772548
  1499.7 47.9 %copy-start.57 = (f32[2,577]{1,0:T(2,128)S(1)}, f32[2,577]{1,0:T(2,128)}, u32[]{:S(2)}) copy-start(f32[2,577]{1,0:T(2,128)} %copy-done.56) | copy-start | bytes 13852
  1499.7 47.9 %copy-start.59 = (f32[2,577]{1,0:T(2,128)S(1)}, f32[2,577]{1,0:T(2,128)}, u32[]{:S(2)}) copy-start(f32[2,577]{1,0:T(2,128)} %copy-done.58) | copy-start | bytes 13852
  1499.7 47.9 %copy-start.73 = (f32[1,1,256]{2,1,0:T(1,128)S(1)}, f32[1,1,256]{2,1,0:T(1,128)}, u32[]{:S(2)}) copy-start(f32[1,1,256]{2,1,0:T(1,128)} %copy-done.72) | copy-start | bytes 3076
  1499.7 67.1 %copy-start.14 = (f32[2,577,256]{2,1,0:T(8,128)S(1)}, f32[2,577,256]{2,1,0:T(8,128)}, u32[]{:S(2)}) copy-start(f32[2,577,256]{2,1,0:T(8,128)} %copy-done.13) | copy-start | bytes 3545092
  1499.7 67.1 %copy-start.76 = (f32[2]{0:T(128)S(1)}, f32[2]{0:T(128)}, u32[]{:S(2)}) copy-start(f32[2]{0:T(128)} %copy-done.75) | copy-start | bytes 28
  1568.7 24.1 %copy-start.60 = (f32[2,8,256]{2,1,0:T(8,128)S(1)}, f32[2,8,256]{2,1,0:T(8,128)}, u32[]{:S(2)}) copy-start(f32[2,8,256]{2,1,0:T(8,128)} %param.22) | copy-start | bytes 49156
  1568.7 24.1 %copy-start.65 = (f32[2,2,8,256]{3,2,1,0:T(8,128)S(1)}, f32[2,2,8,256]{3,2,1,0:T(8,128)}, u32[]{:S(2)}) copy-start(f32[2,2,8,256]{3,2,1,0:T(8,128)} %param.28) | copy-start | bytes 98308
  1568.7 24.8 %copy-start.67 = (f32[2,1024]{1,0:T(2,128)S(1)}, f32[2,1024]{1,0:T(2,128)}, u32[]{:S(2)}) copy-start(f32[2,1024]{1,0:T(2,128)} %param.23) | copy-start | bytes 24580
  1568.7 24.7 %copy-start.70 = (f32[2,2,1024]{2,1,0:T(2,128)S(1)}, f32[2,2,1024]{2,1,0:T(2,128)}, u32[]{:S(2)}) copy-start(f32[2,2,1024]{2,1,0:T(2,128)} %param.29) | copy-start | bytes 49156
  (53 other events, 137.3 us)
Sparse Core Ops, SparseCore 0:
  43.4 26.9 all-gather.26
  133.9 85.4 reduce-scatter.12
  221.9 28.2 all-gather.28
  252.5 27.7 all-gather.30
  323.6 85.3 reduce-scatter.14
  439.8 27.1 all-gather.32
  532.2 85.3 reduce-scatter.16
  619.8 78.4 all-gather.18
  700.7 40.4 all-gather.34
  743.5 27.7 all-gather.36
  787.5 48.2 reduce-scatter.20
  838.0 86.0 reduce-scatter.18
  929.6 51.4 all-gather.20
  1042.3 46.4 reduce-scatter.22
  1112.5 49.0 all-gather.22
  1181.3 46.4 reduce-scatter.24
  1251.9 49.0 all-gather.24
  1304.1 49.2 reduce-scatter.32
  1356.8 51.0 reduce-scatter.34
  1411.6 35.9 reduce-scatter.30
  1451.0 46.0 reduce-scatter.28
  1499.4 48.2 reduce-scatter.26
